TPU v7x, 32 devices: a whole 2x2x4 slice. The times are simulated.
32 devices in a mesh: rows: 8 (over z, y), code: 4 (over x, core).
Axes of the slice: x: 2, y: 2, z: 4, core: 2. Of those that a mesh axis runs over, the one named last changes fastest.
Arguments:
- embedding_vectors: bfloat16 [3072, 256], P('rows'), may hold values from -45.3125 to 45.3125
- codebook: bfloat16 [65536, 256], P(('code', 'rows')), may hold values from -0.38125 to 0.38125
- weights: float32 [3072], P('rows'), may hold values from 0.6 to 4.2
Outputs:
- gradient: float32 [65536, 256], P(('code', 'rows'))
- load: float32 [65536], P(('code', 'rows'))
All inputs are finite; a program needn't handle non-finite values.
Results may differ from a plain program's by a relative error of at most 0.013.
Values may be sent and summed in bfloat16 or wider, within the bound.
No kernel may reach another device: no remote copies, remote signals or barrier semaphores. Data moves between devices by JAX's collectives and lax.ppermute only.
A program may use at most 128 MiB of HBM per device.

v0:
```python
import jax
import jax.numpy as jnp
from jax import lax
from jax.sharding import PartitionSpec as P

ITERS = 3
sharpness_factor = 2.0


def local(embedding_vectors, codebook, weights):
    code_devices = lax.axis_size("code")
    balance = embedding_vectors.shape[0] / (code_devices * codebook.shape[0])
    similarity_table = sharpness_factor * jnp.einsum(
        "nd,kd->nk",
        embedding_vectors,
        lax.all_gather(codebook, "rows", axis=0, tiled=True),
        preferred_element_type=jnp.float32,
    )
    row_peak = lax.pmax(jnp.max(similarity_table, axis=1), "code")
    power_term = jnp.exp(similarity_table - row_peak[:, None])

    def marginal_per_sample(col_scale):
        return lax.psum(jnp.dot(power_term, col_scale, precision=lax.Precision.HIGHEST), "code")

    col_scale = jnp.ones((power_term.shape[1],), jnp.float32)
    row_scale = weights / marginal_per_sample(col_scale)
    for iteration in range(ITERS):
        partial_cols = jnp.dot(row_scale, power_term, precision=lax.Precision.HIGHEST)
        col_scale = balance / lax.psum(partial_cols, "rows")
        row_scale = weights / marginal_per_sample(col_scale)
    transport_plan = power_term * row_scale[:, None] * col_scale[None, :]
    local_mass = jnp.sum(transport_plan, axis=0)
    partial_aggregates = jnp.einsum(
        "nk,nd->kd",
        transport_plan.astype(jnp.bfloat16),
        embedding_vectors,
        preferred_element_type=jnp.float32,
    )
    codeword_sums, code_mass = (
        lax.psum_scatter(partial_aggregates, "rows", scatter_dimension=0, tiled=True),
        lax.psum_scatter(local_mass, "rows", scatter_dimension=0, tiled=True),
    )
    gradient = (code_mass[:, None] * codebook.astype(jnp.float32) - codeword_sums) / balance
    return (gradient, code_mass / balance)


def solution(mesh):
    placed = (P("rows", None), P(("code", "rows"), None), P("rows"))
    return jax.shard_map(
        local,
        mesh=mesh,
        in_specs=placed,
        out_specs=(P(("code", "rows"), None), P(("code", "rows"))),
        check_vma=False,
    )
```

profile of v0, /device:TPU:0, one launch (start us, length us, event | category | flops | bytes accessed | tf_op | source)
XLA Modules:
  0.0 927.6 jit_solution(9325484149887483975)
XLA Ops:
  7.2 0.0 copy-start
  7.2 0.0 all-gather.2.cloned.1.call-start
  7.2 0.7 all-gather.2.cloned.1.call-update
  7.9 0.0 copy-start.2
  7.9 0.0 all-reduce.6.cloned.1.call-start
  8.0 129.8 %all-gather.2.cloned.1.call-done = bf16[16384,256]{1,0:T(8,128)(2,1)} async-done(((bf16[2048,256]{1,0:T(8,128)(2,1)}), bf16[16384,256]{1,0:T(8,128)(2,1)}) %all-gather.2.cloned.1.call-update) | async-done | bytes 8388624 | tf_op jit(solution)/shard_map/all_gather | solution.py:16
  137.8 0.0 copy-done
  137.8 15.2 %fusion.11 = (f32[384]{0:T(512)S(1)}, f32[384,16384]{1,0:T(8,128)}) fusion(bf16[384,256]{1,0:T(8,128)(2,1)S(1)} %copy-done, bf16[16384,256]{1,0:T(8,128)(2,1)} %all-gather.2.cloned.1.call-done), kind=kOutput, calls=%fused_computation.22 | convolution fusion | flops 3233807872 | bytes 33752576 | tf_op jit(solution)/shard_map/nd,kd->nk/dot_general | solution.py:13
  153.0 6.1 pmax.7
  159.1 26.1 %convolution_reduce_fusion.3 = f32[384]{0:T(512)S(1)} fusion(f32[384,16384]{1,0:T(8,128)} %get-tuple-element.5, f32[384]{0:T(512)S(1)} %pmax.7), kind=kOutput, calls=%fused_computation.12 | convolution fusion | flops 81788928 | bytes 25168896 | tf_op jit(solution)/shard_map/dot_general | solution.py:23
  185.2 6.6 psum.49
  191.8 0.0 copy-done.2
  191.8 18.6 %fusion.10 = f32[1,16384]{1,0:T(1,128)} fusion(f32[384,1]{0,1:T(1,128)S(1)} %reshape.10, f32[384,16384]{1,0:T(8,128)} %get-tuple-element.5, f32[384]{0:T(512)S(1)} %pmax.7), kind=kOutput, calls=%fused_computation.21 | convolution fusion | flops 81788928 | bytes 25234432 | tf_op jit(solution)/shard_map/dot_general | solution.py:28
  210.5 0.0 all-reduce.6.cloned.1.call-update
  210.5 0.0 all-reduce.8.cloned.1.call-start
  210.6 66.2 %all-reduce.6.cloned.1.call-done = f32[16384]{0:T(1024)} async-done(((f32[16384]{0:T(1024)}), f32[16384]{0:T(1024)}) %all-reduce.6.cloned.1.call-update) | async-done | bytes 65552 | tf_op jit(solution)/shard_map/psum | solution.py:29
  276.8 0.9 broadcast_divide_fusion.2
  277.6 26.2 %convolution_reduce_fusion.2 = f32[384]{0:T(512)S(1)} fusion(f32[16384,1]{0,1:T(1,128)S(1)} %bitcast.20, f32[384,16384]{1,0:T(8,128)} %get-tuple-element.5, f32[384]{0:T(512)S(1)} %pmax.7), kind=kOutput, calls=%fused_computation.11 | convolution fusion | flops 81788928 | bytes 25234432 | tf_op jit(solution)/shard_map/dot_general | solution.py:23
  303.8 5.8 psum.51
  309.7 18.6 %fusion.9 = f32[1,16384]{1,0:T(1,128)} fusion(f32[384,1]{0,1:T(1,128)S(1)} %reshape.14, f32[384,16384]{1,0:T(8,128)} %get-tuple-element.5, f32[384]{0:T(512)S(1)} %pmax.7), kind=kOutput, calls=%fused_computation.20 | convolution fusion | flops 81788928 | bytes 25234432 | tf_op jit(solution)/shard_map/dot_general | solution.py:28
  328.3 0.0 all-reduce.8.cloned.1.call-update
  328.3 0.0 all-reduce.10.cloned.1.call-start
  328.4 68.8 %all-reduce.8.cloned.1.call-done = f32[16384]{0:T(1024)} async-done(((f32[16384]{0:T(1024)}), f32[16384]{0:T(1024)}) %all-reduce.8.cloned.1.call-update) | async-done | bytes 65552 | tf_op jit(solution)/shard_map/psum | solution.py:29
  397.1 0.9 broadcast_divide_fusion.1
  398.0 26.2 %convolution_reduce_fusion.1 = f32[384]{0:T(512)S(1)} fusion(f32[16384,1]{0,1:T(1,128)S(1)} %bitcast.21, f32[384,16384]{1,0:T(8,128)} %get-tuple-element.5, f32[384]{0:T(512)S(1)} %pmax.7), kind=kOutput, calls=%fused_computation.10 | convolution fusion | flops 81788928 | bytes 25234432 | tf_op jit(solution)/shard_map/dot_general | solution.py:23
  424.2 5.9 psum.53
  430.1 18.6 %fusion.8 = f32[1,16384]{1,0:T(1,128)} fusion(f32[384,1]{0,1:T(1,128)S(1)} %reshape.18, f32[384,16384]{1,0:T(8,128)} %get-tuple-element.5, f32[384]{0:T(512)S(1)} %pmax.7), kind=kOutput, calls=%fused_computation.19 | convolution fusion | flops 81788928 | bytes 25234432 | tf_op jit(solution)/shard_map/dot_general | solution.py:28
  448.7 0.0 all-reduce.10.cloned.1.call-update
  448.7 0.0 all-reduce.12.cloned.1.call-start
  448.8 68.8 %all-reduce.10.cloned.1.call-done = f32[16384]{0:T(1024)} async-done(((f32[16384]{0:T(1024)}), f32[16384]{0:T(1024)}) %all-reduce.10.cloned.1.call-update) | async-done | bytes 65552 | tf_op jit(solution)/shard_map/psum | solution.py:29
  517.6 0.9 broadcast_divide_fusion
  518.4 26.2 %convolution_reduce_fusion = f32[384]{0:T(512)S(1)} fusion(f32[16384,1]{0,1:T(1,128)S(1)} %bitcast.16, f32[384,16384]{1,0:T(8,128)} %get-tuple-element.5, f32[384]{0:T(512)S(1)} %pmax.7), kind=kOutput, calls=%fused_computation.9 | convolution fusion | flops 81788928 | bytes 25234432 | tf_op jit(solution)/shard_map/dot_general | solution.py:23
  544.6 5.7 psum.55
  550.3 11.9 %fusion.1 = f32[16384]{0:T(1024)} fusion(f32[16384]{0:T(1024)S(1)} %broadcast_divide_fusion, f32[384]{0:T(512)S(1)} %div.39, f32[384,16384]{1,0:T(8,128)} %get-tuple-element.5, f32[384]{0:T(512)S(1)} %pmax.7), kind=kLoop, calls=%fused_computation.4 | loop fusion | flops 25149440 | bytes 25299968 | tf_op jit(solution)/shard_map/reduce_sum | solution.py:32
  562.2 0.0 all-reduce.12.cloned.1.call-update
  562.3 0.0 copy-start.3
  562.3 0.0 copy-start.1
  562.3 0.3 reduce-scatter.2.cloned.1.call-start
  562.6 14.9 %fusion.2 = f32[16384,256]{1,0:T(8,128)} fusion(bf16[384,256]{1,0:T(8,128)(2,1)S(1)} %copy-done, f32[16384]{0:T(1024)S(1)} %broadcast_divide_fusion, f32[384]{0:T(512)S(1)} %div.39, f32[384,16384]{1,0:T(8,128)} %get-tuple-element.5, f32[384]{0:T(512)S(1)} %pmax.7), kind=kOutput, calls=%fused_computation.5 | convolution fusion | flops 3246391296 | bytes 42208256 | tf_op jit(solution)/shard_map/nk,nd->kd/dot_general | solution.py:33
  577.5 0.0 reduce-scatter.2.cloned.1.call-update
  577.5 0.0 copy-done.3
  577.6 0.6 dynamic-slice
  578.8 52.3 %all-reduce.12.cloned.1.call-done = f32[16384]{0:T(1024)} async-done(((f32[16384]{0:T(1024)}), f32[16384]{0:T(1024)}) %all-reduce.12.cloned.1.call-update) | async-done | bytes 65552
  631.1 1.3 broadcast_multiply_fusion
  632.4 284.8 %reduce-scatter.2.cloned.1.call-done = f32[2048,256]{1,0:T(8,128)} async-done(((f32[16384,256]{1,0:T(8,128)}), f32[2048,256]{1,0:T(8,128)}) %reduce-scatter.2.cloned.1.call-update) | async-done | bytes 2097168 | tf_op jit(solution)/shard_map/reduce_scatter | solution.py:40
  917.2 0.0 copy-done.1
  917.2 3.3 subtract_multiply_fusion
  (7 shorter events, 0.0 us)
Async XLA Ops:
  7.2 130.6 %copy-start = (bf16[384,256]{1,0:T(8,128)(2,1)S(1)}, bf16[384,256]{1,0:T(8,128)(2,1)}, u32[]{:S(2)}) copy-start(bf16[384,256]{1,0:T(8,128)(2,1)} %param.3) | copy-start | bytes 589828
  7.2 130.6 %all-gather.2.cloned.1.call-start = ((), (), s32[]{:S(2)}) async-start(), calls=%async_computation.1 | async-start | bytes 9437184 | tf_op jit(solution)/shard_map/all_gather | solution.py:16
  7.9 183.9 %copy-start.2 = (f32[384]{0:T(512)S(1)}, f32[384]{0:T(512)}, u32[]{:S(2)}) copy-start(f32[384]{0:T(512)} %param.5) | copy-start | bytes 4612
  7.9 268.8 %all-reduce.6.cloned.1.call-start = ((), (), s32[]{:S(2)}) async-start(), calls=%async_computation.2 | async-start | bytes 131072 | tf_op jit(solution)/shard_map/psum | solution.py:29
  210.5 186.6 %all-reduce.8.cloned.1.call-start = ((), (), s32[]{:S(2)}) async-start(), calls=%async_computation.3 | async-start | bytes 131072 | tf_op jit(solution)/shard_map/psum | solution.py:29
  328.3 189.3 %all-reduce.10.cloned.1.call-start = ((), (), s32[]{:S(2)}) async-start(), calls=%async_computation.4 | async-start | bytes 131072 | tf_op jit(solution)/shard_map/psum | solution.py:29
  448.7 182.4 %all-reduce.12.cloned.1.call-start = ((), (), s32[]{:S(2)}) async-start(), calls=%async_computation.6 | async-start | bytes 131072
  562.3 15.3 %copy-start.3 = (u32[32]{0:T(128)S(1)}, u32[32]{0:T(128)}, u32[]{:S(2)}) copy-start(u32[32]{0:T(128)} %constant.17) | copy-start | bytes 388
  562.3 354.9 %copy-start.1 = (bf16[2048,256]{1,0:T(8,128)(2,1)S(1)}, bf16[2048,256]{1,0:T(8,128)(2,1)}, u32[]{:S(2)}) copy-start(bf16[2048,256]{1,0:T(8,128)(2,1)} %param.4) | copy-start | bytes 3145732
  562.3 354.9 %reduce-scatter.2.cloned.1.call-start = ((), (), s32[]{:S(2)}) async-start(), calls=%async_computation.5 | async-start | bytes 18874368 | tf_op jit(solution)/shard_map/reduce_scatter | solution.py:40
Sparse Core Ops, SparseCore 0:
  10.1 127.6 all-gather.1
  210.6 66.0 all-reduce.5
  328.4 68.6 all-reduce.7
  448.9 68.6 all-reduce.9
  562.4 68.6 all-reduce.11
  634.7 282.4 reduce-scatter.1
where the time goes:
time: 935 us; the launch traced here: 928 us
  waiting for transfers between devices  671 us (72%)
  matrix products  191 us (20%)
  blocking collectives  30.1 us (3%)
  other arithmetic  19.1 us (2%)
  between operations  15.1 us (2%)
    reduce_scatter x1, waiting for transfers between devices, local(): lax.psum_scatter(partial_aggregates, 'rows', scatter_dimension=0, tiled=T...  285 us
    psum x3, waiting for transfers between devices, local(): col_scale = balance / lax.psum(partial_cols, 'rows')  204 us
    all_gather x1, waiting for transfers between devices, local(): lax.all_gather(codebook, 'rows', axis=0, tiled=True)  130 us
    dot_general x4, matrix products, marginal_per_sample(): jnp.dot(power_term, col_scale, precision=lax.Precision.HIGHEST)  105 us
    dot_general x3, matrix products, local(): jnp.dot(row_scale, power_term, precision=lax.Precision.HIGHEST)  55.9 us
    unnamed x7, waiting for transfers between devices  53.1 us
    psum x4, blocking collectives, marginal_per_sample(): lax.psum(jnp.dot(power_term, col_scale, precision=lax.Precision.HIGHEST),...  24 us
  transfers between devices with their start and end apart: 6, of which 6 were waited for; matrix products, arithmetic and copies ran while one was open for 2% of the time, Pallas kernels for 0%

commit v1 on v0

--- a/solution.py
+++ b/solution.py
@@ -7,14 +7,32 @@
 sharpness_factor = 2.0
 
 
+def ring_apply(shard, axis, dim, make, out_dim):
+    ways, here, step = (lax.axis_size(axis), lax.axis_index(axis), shard.shape[dim])
+    results = []
+    for far in range(ways):
+        arriving = (
+            lax.ppermute(shard, axis, [(d, (d + 1) % ways) for d in range(ways)])
+            if far + 1 < ways
+            else shard
+        )
+        results.append(make(shard, (here - far) % ways * step))
+        shard = arriving
+    line = jnp.concatenate(results[::-1], axis=out_dim)
+    return jnp.roll(line, (here + 1) * results[0].shape[out_dim], axis=out_dim)
+
+
 def local(embedding_vectors, codebook, weights):
     code_devices = lax.axis_size("code")
     balance = embedding_vectors.shape[0] / (code_devices * codebook.shape[0])
-    similarity_table = sharpness_factor * jnp.einsum(
-        "nd,kd->nk",
-        embedding_vectors,
-        lax.all_gather(codebook, "rows", axis=0, tiled=True),
-        preferred_element_type=jnp.float32,
+    similarity_table = sharpness_factor * ring_apply(
+        codebook,
+        "rows",
+        0,
+        lambda shard, offset: jnp.einsum(
+            "nd,kd->nk", embedding_vectors, shard, preferred_element_type=jnp.float32
+        ),
+        1,
     )
     row_peak = lax.pmax(jnp.max(similarity_table, axis=1), "code")
     power_term = jnp.exp(similarity_table - row_peak[:, None])

time: 935 us -> 1020 us (1.091)
  waiting for transfers between devices: 671 us -> 715 us
  local copies, waits for them, and re-layouts: 0.63 us -> 18 us
  matrix products: 191 us -> 204 us
    ppermute x0 -> x7, waiting for transfers between devices: none -> 175 us  [ring_apply(): lax.ppermute(shard, axis, [(d, (d + 1) % ways) for d in range(ways)])]
    all_gather x1 -> x0, waiting for transfers between devices: 130 us -> none  [local(): lax.all_gather(codebook, 'rows', axis=0, tiled=True)]
    unnamed x9 -> x24, local copies, waits for them, and re-layouts: 0.61 us -> 16.1 us
    dot_general x1 -> x8, matrix products: 15.2 us -> 22.6 us  [local(): jnp.einsum('nd,kd->nk', embedding_vectors, shard, preferred_element_type=...]
    unnamed x7 -> x6, waiting for transfers between devices: 53.1 us -> 52.2 us
  transfers between devices with their start and end apart: 6 -> 12, of which waited for: 6 -> 12; matrix products, arithmetic and copies ran while one was open for 2% -> 2% of each run, Pallas kernels for 0% -> 0%
where the time goes in v1:
time: 1020 us; the launch traced here: 1010 us
  waiting for transfers between devices  715 us (70%)
  matrix products  204 us (20%)
  other arithmetic  28.8 us (3%)
  blocking collectives  28.7 us (3%)
  local copies, waits for them, and re-layouts  18 us (2%)
  between operations  14.7 us (1%)
    reduce_scatter x1, waiting for transfers between devices, local(): lax.psum_scatter(partial_aggregates, 'rows', scatter_dimension=0, tiled=T...  285 us
    psum x3, waiting for transfers between devices, local(): col_scale = balance / lax.psum(partial_cols, 'rows')  202 us
    ppermute x7, waiting for transfers between devices, ring_apply(): lax.ppermute(shard, axis, [(d, (d + 1) % ways) for d in range(ways)])  175 us
    dot_general x4, matrix products, marginal_per_sample(): jnp.dot(power_term, col_scale, precision=lax.Precision.HIGHEST)  108 us
    dot_general x3, matrix products, local(): jnp.dot(row_scale, power_term, precision=lax.Precision.HIGHEST)  58 us
    unnamed x6, waiting for transfers between devices  52.2 us
    psum x4, blocking collectives, marginal_per_sample(): lax.psum(jnp.dot(power_term, col_scale, precision=lax.Precision.HIGHEST),...  22.8 us
    dot_general x8, matrix products, local(): jnp.einsum('nd,kd->nk', embedding_vectors, shard, preferred_element_type=...  22.6 us
  transfers between devices with their start and end apart: 12, of which 12 were waited for; matrix products, arithmetic and copies ran while one was open for 2% of the time, Pallas kernels for 0%

profile of v1, /device:TPU:0, one launch (start us, length us, event | category | flops | bytes accessed | tf_op | source)
XLA Modules:
  0.0 1012.8 jit_solution(14940308830050471974)
XLA Ops:
  7.2 3.0 collective-permute-start
  10.2 26.4 %collective-permute-done = bf16[2048,256]{1,0:T(8,128)(2,1)S(1)} collective-permute-done((bf16[2048,256]{1,0:T(8,128)(2,1)}, bf16[2048,256]{1,0:T(8,128)(2,1)S(1)}, u32[]{:S(2)}, u32[]{:S(2)}) %collective-permute-start) | collective-permute-done | bytes 1048608 | tf_op jit(solution)/shard_map/ppermute | solution.py:15
  36.7 27.0 %collective-permute-done.1 = bf16[2048,256]{1,0:T(8,128)(2,1)S(1)} collective-permute-done((bf16[2048,256]{1,0:T(8,128)(2,1)S(1)}, bf16[2048,256]{1,0:T(8,128)(2,1)S(1)}, u32[]{:S(2)}, u32[]{:S(2)}) %collective-permute-start.1) | collective-permute-done | bytes 1048608 | tf_op jit(solution)/shard_map/ppermute | solution.py:15
  63.7 26.1 %collective-permute-done.2 = bf16[2048,256]{1,0:T(8,128)(2,1)S(1)} collective-permute-done((bf16[2048,256]{1,0:T(8,128)(2,1)S(1)}, bf16[2048,256]{1,0:T(8,128)(2,1)S(1)}, u32[]{:S(2)}, u32[]{:S(2)}) %collective-permute-start.2) | collective-permute-done | bytes 1048608 | tf_op jit(solution)/shard_map/ppermute | solution.py:15
  89.8 1.0 copy-done.2
  90.8 25.2 %collective-permute-done.3 = bf16[2048,256]{1,0:T(8,128)(2,1)S(1)} collective-permute-done((bf16[2048,256]{1,0:T(8,128)(2,1)S(1)}, bf16[2048,256]{1,0:T(8,128)(2,1)S(1)}, u32[]{:S(2)}, u32[]{:S(2)}) %collective-permute-start.3) | collective-permute-done | bytes 1048608 | tf_op jit(solution)/shard_map/ppermute | solution.py:15
  116.0 1.0 copy-done.4
  117.0 24.3 %collective-permute-done.4 = bf16[2048,256]{1,0:T(8,128)(2,1)S(1)} collective-permute-done((bf16[2048,256]{1,0:T(8,128)(2,1)S(1)}, bf16[2048,256]{1,0:T(8,128)(2,1)S(1)}, u32[]{:S(2)}, u32[]{:S(2)}) %collective-permute-start.4) | collective-permute-done | bytes 1048608 | tf_op jit(solution)/shard_map/ppermute | solution.py:15
  142.2 23.5 %collective-permute-done.5 = bf16[2048,256]{1,0:T(8,128)(2,1)} collective-permute-done((bf16[2048,256]{1,0:T(8,128)(2,1)S(1)}, bf16[2048,256]{1,0:T(8,128)(2,1)}, u32[]{:S(2)}, u32[]{:S(2)}) %collective-permute-start.5) | collective-permute-done | bytes 1048608 | tf_op jit(solution)/shard_map/ppermute | solution.py:15
  165.7 22.7 %collective-permute-done.6 = bf16[2048,256]{1,0:T(8,128)(2,1)} collective-permute-done((bf16[2048,256]{1,0:T(8,128)(2,1)}, bf16[2048,256]{1,0:T(8,128)(2,1)}, u32[]{:S(2)}, u32[]{:S(2)}) %collective-permute-start.6) | collective-permute-done | bytes 1048608 | tf_op jit(solution)/shard_map/ppermute | solution.py:15
  188.5 3.5 constant_dynamic-update-slice_fusion.15
  191.9 3.4 constant_dynamic-update-slice_fusion.14
  195.3 3.4 constant_dynamic-update-slice_fusion.13
  198.8 3.4 constant_dynamic-update-slice_fusion.12
  202.2 2.2 constant_dynamic-update-slice_fusion.11
  204.4 2.2 constant_dynamic-update-slice_fusion.10
  206.6 2.2 constant_dynamic-update-slice_fusion.9
  208.8 2.2 constant_dynamic-update-slice_fusion.8
  211.0 1.8 constant_dynamic-update-slice_fusion.7
  212.8 1.8 constant_dynamic-update-slice_fusion.6
  214.6 1.8 constant_dynamic-update-slice_fusion.5
  216.4 1.8 constant_dynamic-update-slice_fusion.4
  218.2 1.8 constant_dynamic-update-slice_fusion.3
  220.0 1.8 constant_dynamic-update-slice_fusion.2
  221.8 1.8 constant_dynamic-update-slice_fusion.1
  223.6 1.8 constant_dynamic-update-slice_fusion
  225.4 9.4 fusion.2
  234.8 5.9 pmax.7
  240.8 26.9 %convolution_reduce_fusion.3 = f32[384]{0:T(512)S(1)} fusion(f32[384,32768]{1,0:T(8,128)} %constant_dynamic-update-slice_fusion, s32[]{:T(128)S(6)} %select_n.14, f32[384]{0:T(512)S(1)} %pmax.7), kind=kOutput, calls=%fused_computation.13 | convolution fusion | flops 88080384 | bytes 25168900 | tf_op jit(solution)/shard_map/dot_general | solution.py:41
  267.7 5.8 psum.49
  273.5 19.4 %fusion.11 = f32[1,16384]{1,0:T(1,128)} fusion(f32[384,1]{0,1:T(1,128)S(1)} %reshape.10, f32[384,32768]{1,0:T(8,128)} %constant_dynamic-update-slice_fusion, s32[]{:T(128)S(6)} %select_n.14, f32[384]{0:T(512)S(1)} %pmax.7), kind=kOutput, calls=%fused_computation.38 | convolution fusion | flops 88080384 | bytes 25234436 | tf_op jit(solution)/shard_map/dot_general | solution.py:46
  293.1 65.4 %all-reduce.6.cloned.1.call-done = f32[16384]{0:T(1024)} async-done(((f32[16384]{0:T(1024)}), f32[16384]{0:T(1024)}) %all-reduce.6.cloned.1.call-update) | async-done | bytes 65552 | tf_op jit(solution)/shard_map/psum | solution.py:47
  359.4 27.0 %convolution_reduce_fusion.2 = f32[384]{0:T(512)S(1)} fusion(f32[16384,1]{0,1:T(1,128)S(1)} %bitcast.34, f32[384,32768]{1,0:T(8,128)} %constant_dynamic-update-slice_fusion, s32[]{:T(128)S(6)} %select_n.14, f32[384]{0:T(512)S(1)} %pmax.7), kind=kOutput, calls=%fused_computation.12 | convolution fusion | flops 88080384 | bytes 25234436 | tf_op jit(solution)/shard_map/dot_general | solution.py:41
  386.4 5.7 psum.51
  392.1 19.3 %fusion.10 = f32[1,16384]{1,0:T(1,128)} fusion(f32[384,1]{0,1:T(1,128)S(1)} %reshape.14, f32[384,32768]{1,0:T(8,128)} %constant_dynamic-update-slice_fusion, s32[]{:T(128)S(6)} %select_n.14, f32[384]{0:T(512)S(1)} %pmax.7), kind=kOutput, calls=%fused_computation.37 | convolution fusion | flops 88080384 | bytes 25234436 | tf_op jit(solution)/shard_map/dot_general | solution.py:46
  411.9 68.4 %all-reduce.8.cloned.1.call-done = f32[16384]{0:T(1024)} async-done(((f32[16384]{0:T(1024)}), f32[16384]{0:T(1024)}) %all-reduce.8.cloned.1.call-update) | async-done | bytes 65552 | tf_op jit(solution)/shard_map/psum | solution.py:47
  481.1 27.0 %convolution_reduce_fusion.1 = f32[384]{0:T(512)S(1)} fusion(f32[16384,1]{0,1:T(1,128)S(1)} %bitcast.35, f32[384,32768]{1,0:T(8,128)} %constant_dynamic-update-slice_fusion, s32[]{:T(128)S(6)} %select_n.14, f32[384]{0:T(512)S(1)} %pmax.7), kind=kOutput, calls=%fused_computation.11 | convolution fusion | flops 88080384 | bytes 25234436 | tf_op jit(solution)/shard_map/dot_general | solution.py:41
  508.1 5.7 psum.53
  513.8 19.3 %fusion.9 = f32[1,16384]{1,0:T(1,128)} fusion(f32[384,1]{0,1:T(1,128)S(1)} %reshape.18, f32[384,32768]{1,0:T(8,128)} %constant_dynamic-update-slice_fusion, s32[]{:T(128)S(6)} %select_n.14, f32[384]{0:T(512)S(1)} %pmax.7), kind=kOutput, calls=%fused_computation.36 | convolution fusion | flops 88080384 | bytes 25234436 | tf_op jit(solution)/shard_map/dot_general | solution.py:46
  533.4 68.6 %all-reduce.10.cloned.1.call-done = f32[16384]{0:T(1024)} async-done(((f32[16384]{0:T(1024)}), f32[16384]{0:T(1024)}) %all-reduce.10.cloned.1.call-update) | async-done | bytes 65552 | tf_op jit(solution)/shard_map/psum | solution.py:47
  602.9 27.0 %convolution_reduce_fusion = f32[384]{0:T(512)S(1)} fusion(f32[16384,1]{0,1:T(1,128)S(1)} %bitcast.30, f32[384,32768]{1,0:T(8,128)} %constant_dynamic-update-slice_fusion, s32[]{:T(128)S(6)} %select_n.14, f32[384]{0:T(512)S(1)} %pmax.7), kind=kOutput, calls=%fused_computation.10 | convolution fusion | flops 88080384 | bytes 25234436 | tf_op jit(solution)/shard_map/dot_general | solution.py:41
  629.9 5.7 psum.55
  635.5 12.3 %fusion.1 = f32[16384]{0:T(1024)} fusion(f32[16384]{0:T(1024)S(1)} %broadcast_divide_fusion, f32[384]{0:T(512)S(1)} %div.39, f32[384]{0:T(512)S(1)} %pmax.7, f32[384,32768]{1,0:T(8,128)} %constant_dynamic-update-slice_fusion, s32[]{:T(128)S(6)} %select_n.14), kind=kLoop, calls=%fused_computation.4 | loop fusion | flops 31440896 | bytes 25299972 | tf_op jit(solution)/shard_map/reduce_sum | solution.py:50
  647.9 15.4 %fusion.3 = f32[16384,256]{1,0:T(8,128)} fusion(bf16[384,256]{1,0:T(8,128)(2,1)S(1)} %copy-done, f32[16384]{0:T(1024)S(1)} %broadcast_divide_fusion, f32[384]{0:T(512)S(1)} %div.39, f32[384,32768]{1,0:T(8,128)} %constant_dynamic-update-slice_fusion, s32[]{:T(128)S(6)} %select_n.14, f32[384]{0:T(512)S(1)} %pmax.7), kind=kOutput, calls=%fused_computation.6 | convolution fusion | flops 3252682752 | bytes 42208260 | tf_op jit(solution)/shard_map/nk,nd->kd/dot_general | solution.py:51
  664.6 52.1 %all-reduce.12.cloned.1.call-done = f32[16384]{0:T(1024)} async-done(((f32[16384]{0:T(1024)}), f32[16384]{0:T(1024)}) %all-reduce.12.cloned.1.call-update) | async-done | bytes 65552
  716.7 1.3 broadcast_multiply_fusion
  718.0 284.9 %reduce-scatter.2.cloned.1.call-done = f32[2048,256]{1,0:T(8,128)} async-done(((f32[16384,256]{1,0:T(8,128)}), f32[2048,256]{1,0:T(8,128)}) %reduce-scatter.2.cloned.1.call-update) | async-done | bytes 2097168 | tf_op jit(solution)/shard_map/reduce_scatter | solution.py:58
  1002.9 3.2 subtract_multiply_fusion
  (41 shorter events, 5.3 us)
Async XLA Ops:
  7.2 181.3 %copy-start = (bf16[384,256]{1,0:T(8,128)(2,1)S(1)}, bf16[384,256]{1,0:T(8,128)(2,1)}, u32[]{:S(2)}) copy-start(bf16[384,256]{1,0:T(8,128)(2,1)} %param.3) | copy-start | bytes 589828
  7.2 351.4 %all-reduce.6.cloned.1.call-start = ((), (), s32[]{:S(2)}) async-start(), calls=%async_computation.1 | async-start | bytes 131072 | tf_op jit(solution)/shard_map/psum | solution.py:47
  7.2 29.4 %collective-permute-start = (bf16[2048,256]{1,0:T(8,128)(2,1)}, bf16[2048,256]{1,0:T(8,128)(2,1)S(1)}, u32[]{:S(2)}, u32[]{:S(2)}) collective-permute-start(bf16[2048,256]{1,0:T(8,128)(2,1)} %param.4), channel_id=1, source_target_pairs={{0,4},{4,8},{8,12},{12,16},{16,20},{20,24},{24,28},{28,0},{1,5},{5... | collective-permute-start | bytes 3145736 | tf_op jit(solution)/shard_map/ppermute | solution.py:15
  36.7 27.0 %collective-permute-start.1 = (bf16[2048,256]{1,0:T(8,128)(2,1)S(1)}, bf16[2048,256]{1,0:T(8,128)(2,1)S(1)}, u32[]{:S(2)}, u32[]{:S(2)}) collective-permute-start(bf16[2048,256]{1,0:T(8,128)(2,1)S(1)} %collective-permute-done), channel_id=1, source_target_pairs={{0,4},{4,8},{8,12},{12,16},{16,20},{20,24},{24,28},{28,0},{1,5},{5... | collective-permute-start | bytes 3145736 | tf_op jit(solution)/shard_map/ppermute | solution.py:15
  63.7 26.1 %collective-permute-start.2 = (bf16[2048,256]{1,0:T(8,128)(2,1)S(1)}, bf16[2048,256]{1,0:T(8,128)(2,1)S(1)}, u32[]{:S(2)}, u32[]{:S(2)}) collective-permute-start(bf16[2048,256]{1,0:T(8,128)(2,1)S(1)} %collective-permute-done.1), channel_id=1, source_target_pairs={{0,4},{4,8},{8,12},{12,16},{16,20},{20,24},{24,28},{28,0},{1,5},{5... | collective-permute-start | bytes 3145736 | tf_op jit(solution)/shard_map/ppermute | solution.py:15
  89.8 1.0 copy-start.2
  90.8 25.2 %collective-permute-start.3 = (bf16[2048,256]{1,0:T(8,128)(2,1)S(1)}, bf16[2048,256]{1,0:T(8,128)(2,1)S(1)}, u32[]{:S(2)}, u32[]{:S(2)}) collective-permute-start(bf16[2048,256]{1,0:T(8,128)(2,1)S(1)} %collective-permute-done.2), channel_id=1, source_target_pairs={{0,4},{4,8},{8,12},{12,16},{16,20},{20,24},{24,28},{28,0},{1,5},{5... | collective-permute-start | bytes 3145736 | tf_op jit(solution)/shard_map/ppermute | solution.py:15
  116.0 1.0 copy-start.4
  117.0 24.3 %collective-permute-start.4 = (bf16[2048,256]{1,0:T(8,128)(2,1)S(1)}, bf16[2048,256]{1,0:T(8,128)(2,1)S(1)}, u32[]{:S(2)}, u32[]{:S(2)}) collective-permute-start(bf16[2048,256]{1,0:T(8,128)(2,1)S(1)} %collective-permute-done.3), channel_id=1, source_target_pairs={{0,4},{4,8},{8,12},{12,16},{16,20},{20,24},{24,28},{28,0},{1,5},{5... | collective-permute-start | bytes 3145736 | tf_op jit(solution)/shard_map/ppermute | solution.py:15
  141.3 1.0 copy-start.5
  142.2 23.5 %collective-permute-start.5 = (bf16[2048,256]{1,0:T(8,128)(2,1)S(1)}, bf16[2048,256]{1,0:T(8,128)(2,1)}, u32[]{:S(2)}, u32[]{:S(2)}) collective-permute-start(bf16[2048,256]{1,0:T(8,128)(2,1)S(1)} %collective-permute-done.4), channel_id=1, source_target_pairs={{0,4},{4,8},{8,12},{12,16},{16,20},{20,24},{24,28},{28,0},{1,5},{5... | collective-permute-start | bytes 3145736 | tf_op jit(solution)/shard_map/ppermute | solution.py:15
  165.7 22.8 %collective-permute-start.6 = (bf16[2048,256]{1,0:T(8,128)(2,1)}, bf16[2048,256]{1,0:T(8,128)(2,1)}, u32[]{:S(2)}, u32[]{:S(2)}) collective-permute-start(bf16[2048,256]{1,0:T(8,128)(2,1)} %collective-permute-done.5), channel_id=1, source_target_pairs={{0,4},{4,8},{8,12},{12,16},{16,20},{20,24},{24,28},{28,0},{1,5},{5... | collective-permute-start | bytes 3145736 | tf_op jit(solution)/shard_map/ppermute | solution.py:15
  165.7 36.5 %copy-start.3 = (bf16[2048,256]{1,0:T(8,128)(2,1)S(1)}, bf16[2048,256]{1,0:T(8,128)(2,1)}, u32[]{:S(2)}) copy-start(bf16[2048,256]{1,0:T(8,128)(2,1)} %copy-done.2) | copy-start | bytes 3145732
  165.7 43.1 %copy-start.1 = (bf16[2048,256]{1,0:T(8,128)(2,1)S(1)}, bf16[2048,256]{1,0:T(8,128)(2,1)}, u32[]{:S(2)}) copy-start(bf16[2048,256]{1,0:T(8,128)(2,1)} %param.4) | copy-start | bytes 3145732
  225.4 48.1 %copy-start.6 = (f32[384]{0:T(512)S(1)}, f32[384]{0:T(512)}, u32[]{:S(2)}) copy-start(f32[384]{0:T(512)} %param.5) | copy-start | bytes 4612
  292.9 187.4 %all-reduce.8.cloned.1.call-start = ((), (), s32[]{:S(2)}) async-start(), calls=%async_computation.2 | async-start | bytes 131072 | tf_op jit(solution)/shard_map/psum | solution.py:47
  411.4 190.6 %all-reduce.10.cloned.1.call-start = ((), (), s32[]{:S(2)}) async-start(), calls=%async_computation.3 | async-start | bytes 131072 | tf_op jit(solution)/shard_map/psum | solution.py:47
  533.2 183.5 %all-reduce.12.cloned.1.call-start = ((), (), s32[]{:S(2)}) async-start(), calls=%async_computation.5 | async-start | bytes 131072
  647.9 15.4 %copy-start.7 = (u32[32]{0:T(128)S(1)}, u32[32]{0:T(128)}, u32[]{:S(2)}) copy-start(u32[32]{0:T(128)} %constant.49) | copy-start | bytes 388
  647.9 355.0 %reduce-scatter.2.cloned.1.call-start = ((), (), s32[]{:S(2)}) async-start(), calls=%async_computation.4 | async-start | bytes 18874368 | tf_op jit(solution)/shard_map/reduce_scatter | solution.py:58
Sparse Core Ops, SparseCore 0:
  293.0 65.5 all-reduce.5
  411.6 68.6 all-reduce.7
  533.3 68.6 all-reduce.9
  648.0 68.6 all-reduce.11
  720.3 282.4 reduce-scatter.1
